TPU v7x, 32 devices: a whole 2x2x4 slice. The times are simulated.
32 devices in a mesh: rows: 16 (over z, y, x), cols: 2 (over core).
Axes of the slice: x: 2, y: 2, z: 4, core: 2. Of those that a mesh axis runs over, the one named last changes fastest.
Arguments:
- points: bfloat16 [20480, 512], P('rows', 'cols'), may hold values from -6 to 6
- factor: bfloat16 [20480, 1024], P('rows', 'cols'), may hold values from -2 to 2
- weights: float32 [20480], P('rows'), may hold values from -4 to 4
- pivot_slots: int32 [4, 128], replicated, may hold values from 0 to 1279, as said below
- pivot_owners: int32 [4, 128], replicated, may hold values from 0 to 15
Outputs:
- new_panels: bfloat16 [20480, 512], P('rows', 'cols')
- gram_old: float32 [512, 1024], P('rows', 'cols')
- gram_new: float32 [512, 512], P('rows', 'cols')
Inputs may be any that keep to these rules, and one draw needn't show every extreme that they name: Pivot k of panel q is row pivot_slots[q,k] of the block of device pivot_owners[q,k]; the pivots of all panels together are distinct points.
All inputs are finite; a program needn't handle non-finite values.
Results may differ from a plain program's by a relative error of at most 0.009.
Values may be sent and summed in bfloat16 or wider, within the bound.
A program may use at most 64 MiB of HBM per device.

v0:
```python
import math
import jax
import jax.numpy as jnp
from jax import lax
from jax.sharding import PartitionSpec as P

F = 512
R = 1024
RIDGE_LEVEL = 1.0


def body(points, factor, weights, pivot_slots, pivot_owners):
    rows_here = points.shape[0]
    panel = pivot_slots.shape[1]
    panel_count = pivot_slots.shape[0]
    device = lax.axis_index("rows")
    column = lax.axis_index("cols")
    halves = lax.axis_size("cols")
    total_rows = rows_here * lax.axis_size("rows")
    identity = jnp.eye(panel, dtype=jnp.float32)
    half_rows = rows_here // halves
    full_points, full_factor = (
        lax.all_to_all(points, "cols", split_axis=0, concat_axis=1, tiled=True),
        lax.all_to_all(factor, "cols", split_axis=0, concat_axis=1, tiled=True),
    )
    local_ids = device * rows_here + column * half_rows + jnp.arange(half_rows, dtype=jnp.int32)
    local_norms = jnp.sum(jnp.square(full_points.astype(jnp.float32)), axis=1)
    built_half = jnp.zeros((half_rows, panel_count * panel), jnp.bfloat16)
    for index in range(panel_count):
        slots = pivot_slots[index]
        owners = pivot_owners[index]
        pivot_ids = owners * rows_here + slots
        chosen = ((owners == device) & (slots // half_rows == column))[:, None]
        local_slots = slots % half_rows
        sel_points = jnp.where(
            chosen, jnp.take(full_points, local_slots, axis=0).astype(jnp.float32), 0.0
        )
        sel_factor = jnp.where(
            chosen, jnp.take(full_factor, local_slots, axis=0).astype(jnp.float32), 0.0
        )
        sel_built = jnp.where(
            chosen, jnp.take(built_half, local_slots, axis=0).astype(jnp.float32), 0.0
        )
        sel_points, sel_factor, sel_built = lax.psum(
            (sel_points, sel_factor, sel_built), ("rows", "cols")
        )
        piv_norms = jnp.sum(jnp.square(sel_points), axis=1)
        piv_points = sel_points.astype(jnp.bfloat16)
        piv_factor = sel_factor.astype(jnp.bfloat16)
        piv_built = sel_built.astype(jnp.bfloat16)
        cross = jnp.dot(full_points, piv_points.T, preferred_element_type=jnp.float32)
        dist = local_norms[:, None] + piv_norms[None, :] - 2.0 * cross
        schur = jnp.dot(full_factor, piv_factor.T, preferred_element_type=jnp.float32)
        block_dist = (
            piv_norms[:, None]
            + piv_norms[None, :]
            - 2.0 * jnp.dot(piv_points, piv_points.T, preferred_element_type=jnp.float32)
        )
        block_schur = jnp.dot(piv_factor, piv_factor.T, preferred_element_type=jnp.float32)
        ridge = jnp.where(local_ids[:, None] == pivot_ids[None, :], RIDGE_LEVEL, 0.0)
        columns = (
            jnp.exp(-dist / F)
            + ridge
            + schur / (3.0 * R)
            - jnp.dot(built_half, piv_built.T, preferred_element_type=jnp.float32)
        )
        block = (
            jnp.exp(-block_dist / F)
            + RIDGE_LEVEL * identity
            + block_schur / (3.0 * R)
            - jnp.dot(piv_built, piv_built.T, preferred_element_type=jnp.float32)
        )
        lower = jnp.linalg.cholesky(block)
        inverse = lax.linalg.triangular_solve(lower, identity, left_side=True, lower=True)
        fresh = jnp.dot(columns, inverse.T, precision=lax.Precision.HIGHEST).astype(jnp.bfloat16)
        built_half = built_half.at[:, index * panel : (index + 1) * panel].set(fresh)
    built = lax.all_gather(built_half, "cols", axis=0, tiled=True)
    width = built.shape[1] // halves
    own_columns = lax.dynamic_slice_in_dim(built, column * width, width, 1)
    weighted = (built.astype(jnp.float32) * weights[:, None]).astype(jnp.bfloat16)
    dims = (((0,), (0,)), ((), ()))
    old_part = lax.dot_general(weighted, factor, dims, preferred_element_type=jnp.float32)
    new_part = lax.dot_general(weighted, own_columns, dims, preferred_element_type=jnp.float32)
    old_full, new_full = lax.psum((old_part, new_part), "rows")
    out_rows = old_part.shape[0] // lax.axis_size("rows")
    old_sum = lax.dynamic_slice_in_dim(old_full, device * out_rows, out_rows, 0)
    new_sum = lax.dynamic_slice_in_dim(new_full, device * out_rows, out_rows, 0)
    scale = panel / math.sqrt(total_rows)
    return (own_columns, old_sum * scale, new_sum * scale)


def solution(mesh):
    return jax.shard_map(
        body,
        mesh=mesh,
        in_specs=(P("rows", "cols"), P("rows", "cols"), P("rows"), P(), P()),
        out_specs=(P("rows", "cols"), P("rows", "cols"), P("rows", "cols")),
        check_vma=False,
    )
```

profile of v0, /device:TPU:0, one launch (start us, length us, event | category | flops | bytes accessed | tf_op | source)
XLA Modules:
  0.0 558.6 jit_solution(13490840416334126539)
XLA Ops:
  7.2 3.5 all-to-all-start
  12.5 3.6 all-to-all-start.1
  20.2 1.6 gather_fusion.2
  30.1 1.7 gather_fusion.1
  33.4 1.7 gather_fusion.7
  37.3 1.9 convert_select_fusion.2
  39.3 1.9 convert_select_fusion.1
  42.1 50.2 %all-reduce.17 = (bf16[128,1024]{1,0:T(8,128)(2,1)S(1)}, bf16[128,512]{1,0:T(8,128)(2,1)S(1)}) all-reduce(f32[128,1024]{1,0:T(8,128)S(1)} %convert_select_fusion.3, f32[128,512]{1,0:T(8,128)} %get-tuple-element.94), channel_id=1, replica_groups=mesh['rows'=16,'cols'=2] {'rows','cols'}, use_global_device_ids=true, to_apply=%region_4.7 | all-reduce | flops 196608 | bytes 1179648 | tf_op jit(solution)/shard_map/psum | solution.py:44
  95.4 66.1 %all-reduce.14.cloned.1.call-done = (f32[128,512]{1,0:T(8,128)}, f32[128,512]{1,0:T(8,128)}, f32[128,512]{1,0:T(8,128)}, f32[128,512]{1,0:T(8,128)}) async-done(((f32[128,512]{1,0:T(8,128)}, f32[128,512]{1,0:T(8,128)}, f32[128,512]{1,0:T(8,128)}, f32[128,512]{1,0:T(8,128)}), (f32[128,512]{1,0:T(8,128)}, f32[128,512]{1,0:T(8,128)}, f32[128,512]{1,0:T(8,128)}, ...) | async-done | bytes 1048592 | tf_op jit(solution)/shard_map/psum | solution.py:44
  164.2 11.7 %cholesky.74 = f32[128,128]{1,0:T(8,128)S(1)} custom-call(f32[128,128]{1,0:T(8,128)S(1)} %fusion.93), custom_call_target="Cholesky" | custom-call | tf_op jit(solution)/shard_map/jit(cholesky)/cholesky | solution.py:73
  177.2 9.8 %custom-call.8 = f32[1,128,128]{1,2,0:T(8,128)S(1)} custom-call(f32[1,128,128]{2,1,0:T(8,128)S(1)} %fusion.82), custom_call_target="InvertDiagBlocksLowerTriangular" | custom-call | tf_op jit(solution)/shard_map/triangular_solve/custom-call.0 | solution.py:74
  190.3 47.6 %all-reduce.18 = (bf16[128,1024]{1,0:T(8,128)(2,1)S(1)}, bf16[128,512]{1,0:T(8,128)(2,1)S(1)}) all-reduce(f32[128,1024]{1,0:T(8,128)} %convert_select_fusion.2, f32[128,512]{1,0:T(8,128)S(1)} %convert_select_fusion.8), channel_id=1, replica_groups=mesh['rows'=16,'cols'=2] {'rows','cols'}, use_global_device_ids=true, to_apply=%region_11.16 | all-reduce | flops 196608 | bytes 1179648 | tf_op jit(solution)/shard_map/psum | solution.py:44
  240.1 11.7 %cholesky.85 = f32[128,128]{1,0:T(8,128)S(1)} custom-call(f32[128,128]{1,0:T(8,128)S(1)} %fusion.91), custom_call_target="Cholesky" | custom-call | tf_op jit(solution)/shard_map/jit(cholesky)/cholesky | solution.py:73
  253.1 9.8 %custom-call.9 = f32[1,128,128]{1,2,0:T(8,128)S(1)} custom-call(f32[1,128,128]{2,1,0:T(8,128)S(1)} %fusion.83), custom_call_target="InvertDiagBlocksLowerTriangular" | custom-call | tf_op jit(solution)/shard_map/triangular_solve/custom-call.0 | solution.py:74
  267.1 45.8 %all-reduce.19 = (bf16[128,1024]{1,0:T(8,128)(2,1)S(1)}, bf16[128,512]{1,0:T(8,128)(2,1)}) all-reduce(f32[128,1024]{1,0:T(8,128)} %convert_select_fusion.1, f32[128,512]{1,0:T(8,128)S(1)} %convert_select_fusion.6), channel_id=1, replica_groups=mesh['rows'=16,'cols'=2] {'rows','cols'}, use_global_device_ids=true, to_apply=%region_16.21 | all-reduce | flops 196608 | bytes 1179648 | tf_op jit(solution)/shard_map/psum | solution.py:44
  314.5 11.7 %cholesky.96 = f32[128,128]{1,0:T(8,128)S(1)} custom-call(f32[128,128]{1,0:T(8,128)S(1)} %fusion.89), custom_call_target="Cholesky" | custom-call | tf_op jit(solution)/shard_map/jit(cholesky)/cholesky | solution.py:73
  327.6 9.8 %custom-call.10 = f32[1,128,128]{1,2,0:T(8,128)S(1)} custom-call(f32[1,128,128]{2,1,0:T(8,128)S(1)} %fusion.84), custom_call_target="InvertDiagBlocksLowerTriangular" | custom-call | tf_op jit(solution)/shard_map/triangular_solve/custom-call.0 | solution.py:74
  341.3 47.0 %all-reduce.20 = (bf16[128,1024]{1,0:T(8,128)(2,1)S(1)}, bf16[128,512]{1,0:T(8,128)(2,1)}) all-reduce(f32[128,1024]{1,0:T(8,128)} %convert_select_fusion, f32[128,512]{1,0:T(8,128)S(1)} %convert_select_fusion.4), channel_id=1, replica_groups=mesh['rows'=16,'cols'=2] {'rows','cols'}, use_global_device_ids=true, to_apply=%region_20.25 | all-reduce | flops 196608 | bytes 1179648 | tf_op jit(solution)/shard_map/psum | solution.py:44
  389.9 11.7 %cholesky.107 = f32[128,128]{1,0:T(8,128)S(1)} custom-call(f32[128,128]{1,0:T(8,128)S(1)} %fusion.87), custom_call_target="Cholesky" | custom-call | tf_op jit(solution)/shard_map/jit(cholesky)/cholesky | solution.py:73
  403.0 9.8 %custom-call.11 = f32[1,128,128]{1,2,0:T(8,128)S(1)} custom-call(f32[1,128,128]{2,1,0:T(8,128)S(1)} %fusion.85), custom_call_target="InvertDiagBlocksLowerTriangular" | custom-call | tf_op jit(solution)/shard_map/triangular_solve/custom-call.0 | solution.py:74
  415.2 8.4 %all-gather.2.cloned.1.call-done = bf16[1280,512]{1,0:T(8,128)(2,1)} async-done(((bf16[640,512]{1,0:T(8,128)(2,1)}), bf16[1280,512]{1,0:T(8,128)(2,1)}) %all-gather.2.cloned.1.call-update) | async-done | bytes 1310736 | tf_op jit(solution)/shard_map/all_gather | solution.py:77
  424.8 3.5 fusion.63
  428.3 1.7 fusion.62
  430.0 119.0 %all-reduce.16.cloned.1.call-done = (f32[512,512]{1,0:T(8,128)}, f32[512,256]{1,0:T(8,128)}) async-done(((f32[512,512]{1,0:T(8,128)}, f32[512,256]{1,0:T(8,128)}), (f32[512,512]{1,0:T(8,128)}, f32[512,256]{1,0:T(8,128)})) %all-reduce.16.cloned.1.call-update) | async-done | bytes 1572880 | tf_op jit(solution)/shard_map/psum | solution.py:84
  (177 shorter events, 52.4 us)
Async XLA Ops:
  7.2 3.6 copy-start.25
  7.2 3.6 copy-start.23
  7.2 5.4 all-to-all-start
  11.4 27.9 %copy-start.17 = (pred[128]{0:T(512)(128)(4,1)}, pred[128]{0:T(512)(128)(4,1)S(1)}, u32[]{:S(2)}) copy-start(pred[128]{0:T(512)(128)(4,1)S(1)} %get-tuple-element.89) | copy-start | bytes 388
  11.4 29.8 %copy-start.15 = (pred[128]{0:T(512)(128)(4,1)}, pred[128]{0:T(512)(128)(4,1)S(1)}, u32[]{:S(2)}) copy-start(pred[128]{0:T(512)(128)(4,1)S(1)} %get-tuple-element.91) | copy-start | bytes 388
  11.4 4.9 copy-start.28
  12.5 15.0 %all-to-all-start.1 = ((bf16[2,640,512]{2,1,0:T(8,128)(2,1)}), bf16[2,640,512]{2,1,0:T(8,128)(2,1)S(1)}, u32[]{:S(2)}, u32[]{:S(2)}) async-start(bf16[2,640,512]{2,1,0:T(8,128)(2,1)} %bitcast.251), calls=%async_computation.1 | async-start | bytes 2621440 | tf_op jit(solution)/shard_map/all_to_all | solution.py:24
  16.2 145.3 %all-reduce.14.cloned.1.call-start = ((), (), s32[]{:S(2)}) async-start(), calls=%async_computation.3 | async-start | bytes 2097152 | tf_op jit(solution)/shard_map/psum | solution.py:44
  21.8 3.1 copy-start.13
  21.8 3.1 copy-start.31
  21.8 3.1 copy-start.33
  22.5 9.3 %copy-start.29 = (s32[1024]{0:T(1024)}, s32[1024]{0:T(1024)S(1)}, u32[]{:S(2)}) copy-start(s32[1024]{0:T(1024)S(1)} %pad_clamp_fusion.2) | copy-start | bytes 12292
  26.9 396.7 %all-gather.2.cloned.1.call-start = ((), (), s32[]{:S(2)}) async-start(), calls=%async_computation.2 | async-start | bytes 1966080 | tf_op jit(solution)/shard_map/all_gather | solution.py:77
  95.4 91.9 %copy-start.37 = (s32[128]{0:T(128)S(1)}, s32[128]{0:T(128)}, u32[]{:S(2)}) copy-start(s32[128]{0:T(128)} %get-tuple-element.78) | copy-start | bytes 1540
  161.5 25.9 %copy-start.5 = (f32[128,512]{1,0:T(8,128)S(1)}, f32[128,512]{1,0:T(8,128)}, u32[]{:S(2)}) copy-start(f32[128,512]{1,0:T(8,128)} %get-tuple-element.63) | copy-start | bytes 786436
  239.4 23.8 %copy-start.36 = (s32[128]{0:T(128)S(1)}, s32[128]{0:T(128)}, u32[]{:S(2)}) copy-start(s32[128]{0:T(128)} %get-tuple-element.79) | copy-start | bytes 1540
  314.2 24.5 %copy-start.10 = (bf16[128,512]{1,0:T(8,128)(2,1)S(1)}, bf16[128,512]{1,0:T(8,128)(2,1)}, u32[]{:S(2)}) copy-start(bf16[128,512]{1,0:T(8,128)(2,1)} %get-tuple-element.58) | copy-start | bytes 393220
  389.1 24.0 %copy-start.35 = (s32[128]{0:T(128)S(1)}, s32[128]{0:T(128)}, u32[]{:S(2)}) copy-start(s32[128]{0:T(128)} %get-tuple-element.77) | copy-start | bytes 1540
  389.6 23.9 %copy-start.8 = (bf16[128,512]{1,0:T(8,128)(2,1)S(1)}, bf16[128,512]{1,0:T(8,128)(2,1)}, u32[]{:S(2)}) copy-start(bf16[128,512]{1,0:T(8,128)(2,1)} %get-tuple-element.56) | copy-start | bytes 393220
  413.8 10.9 %copy-start.6 = (bf16[1280,512]{1,0:T(8,128)(2,1)S(1)}, bf16[1280,512]{1,0:T(8,128)(2,1)}, u32[]{:S(2)}) copy-start(bf16[1280,512]{1,0:T(8,128)(2,1)} %param.21) | copy-start | bytes 3932164
  413.8 10.9 %copy-start.38 = (f32[1280]{0:T(1024)S(1)}, f32[1280]{0:T(1024)}, u32[]{:S(2)}) copy-start(f32[1280]{0:T(1024)} %param.22) | copy-start | bytes 15364
  415.1 133.8 %all-reduce.16.cloned.1.call-start = ((), (), s32[]{:S(2)}) async-start(), calls=%async_computation.4 | async-start | bytes 3145728 | tf_op jit(solution)/shard_map/psum | solution.py:84
  424.7 3.6 copy-start.11
  424.7 3.6 copy-start.14
  (20 other events, 32.6 us)
Sparse Core Ops, SparseCore 0:
  27.0 134.4 all-reduce.13
  415.3 8.2 all-gather.1
  430.1 118.8 all-reduce.15
where the time goes:
time: 563 us; the launch traced here: 559 us
  waiting for transfers between devices  195 us (35%)
  blocking collectives  191 us (34%)
  other arithmetic  110 us (20%)
  local copies, waits for them, and re-layouts  20.8 us (4%)
  matrix products  20.8 us (4%)
  between operations  14.9 us (3%)
  starting transfers between devices  7.27 us (1%)
    psum x4, blocking collectives, body(): lax.psum((sel_points, sel_factor, sel_built), ('rows', 'cols'))  191 us
    psum x1, waiting for transfers between devices, body(): old_full, new_full = lax.psum((old_part, new_part), 'rows')  119 us
    psum x1, waiting for transfers between devices, body(): lax.psum((sel_points, sel_factor, sel_built), ('rows', 'cols'))  66.1 us
    another operation x12, other arithmetic, body(): lower = jnp.linalg.cholesky(block)  49.6 us
    another operation x8, other arithmetic, body(): lax.linalg.triangular_solve(lower, identity, left_side=True, lower=True)  41.9 us
  transfers between devices with their start and end apart: 5, of which 4 were waited for; matrix products, arithmetic and copies ran while one was open for 5% of the time, Pallas kernels for 0%

commit v1 on v0

--- a/solution.py
+++ b/solution.py
@@ -41,9 +41,11 @@
         sel_built = jnp.where(
             chosen, jnp.take(built_half, local_slots, axis=0).astype(jnp.float32), 0.0
         )
-        sel_points, sel_factor, sel_built = lax.psum(
-            (sel_points, sel_factor, sel_built), ("rows", "cols")
-        )
+
+        def carry_the_counts(x_part):
+            return jax.lax.psum(jax.lax.psum(x_part, axis_name="cols"), axis_name="rows")
+
+        sel_points, sel_factor, sel_built = carry_the_counts((sel_points, sel_factor, sel_built))
         piv_norms = jnp.sum(jnp.square(sel_points), axis=1)
         piv_points = sel_points.astype(jnp.bfloat16)
         piv_factor = sel_factor.astype(jnp.bfloat16)

time: 563 us -> 759 us (1.35)
  blocking collectives: 191 us -> 351 us
  waiting for transfers between devices: 195 us -> 223 us
  other arithmetic: 110 us -> 118 us
    psum x4, blocking collectives: 191 us -> 351 us  [carry_the_counts(): jax.lax.psum(jax.lax.psum(x_part, axis_name='cols'), axis_name='rows')]
    psum x1 -> x5, waiting for transfers between devices: 66.1 us -> 97 us  [the longest x4 65.2 us: carry_the_counts(): jax.lax.psum(x_part, axis_name='cols')]
  transfers between devices with their start and end apart: 5 -> 9, of which waited for: 4 -> 8; matrix products, arithmetic and copies ran while one was open for 5% -> 2% of each run, Pallas kernels for 0% -> 0%
where the time goes in v1:
time: 759 us; the launch traced here: 754 us
  blocking collectives  351 us (46%)
  waiting for transfers between devices  223 us (29%)
  other arithmetic  118 us (16%)
  matrix products  20.5 us (3%)
  local copies, waits for them, and re-layouts  19.3 us (3%)
  between operations  15.1 us (2%)
    psum x4, blocking collectives, carry_the_counts(): jax.lax.psum(jax.lax.psum(x_part, axis_name='cols'), axis_name='rows')  351 us
    psum x1, waiting for transfers between devices, body(): old_full, new_full = lax.psum((old_part, new_part), 'rows')  119 us
    psum x4, waiting for transfers between devices, carry_the_counts(): jax.lax.psum(x_part, axis_name='cols')  65.2 us
    another operation x12, other arithmetic, body(): lower = jnp.linalg.cholesky(block)  52.7 us
    another operation x8, other arithmetic, body(): lax.linalg.triangular_solve(lower, identity, left_side=True, lower=True)  44.8 us
    psum x1, waiting for transfers between devices, carry_the_counts(): jax.lax.psum(jax.lax.psum(x_part, axis_name='cols'), axis_name='rows')  31.8 us
  transfers between devices with their start and end apart: 9, of which 8 were waited for; matrix products, arithmetic and copies ran while one was open for 2% of the time, Pallas kernels for 0%

profile of v1, /device:TPU:0, one launch (start us, length us, event | category | flops | bytes accessed | tf_op | source)
XLA Modules:
  0.0 753.7 jit_solution(13155407943061798179)
XLA Ops:
  7.2 3.5 all-to-all-start
  12.5 3.6 all-to-all-start.1
  28.0 1.7 convert_select_fusion.11
  33.1 21.9 %all-reduce.32.cloned.1.call-done = (f32[128,1024]{1,0:T(8,128)}, f32[128,512]{1,0:T(8,128)}, f32[128,512]{1,0:T(8,128)}, f32[128,512]{1,0:T(8,128)}, f32[128,512]{1,0:T(8,128)}, /*index=5*/f32[128,512]{1,0:T(8,128)}) async-done(((f32[128,1024]{1,0:T(8,128)}, f32[128,512]{1,0:T(8,128)}, f32[128,512]{1,0:T(8,128)}, f32[128,512]{1,0:T(8,128)}, f32[128,512]{1,0:T(8,128)}, /*index=5*/f32[128,512]{1,0:T(8,128)}), ...) | async-done | bytes 1835024 | tf_op jit(solution)/shard_map/psum | solution.py:46
  56.0 89.8 %all-reduce.33 = (bf16[128,1024]{1,0:T(8,128)(2,1)S(1)}, bf16[128,512]{1,0:T(8,128)(2,1)S(1)}) all-reduce(f32[128,1024]{1,0:T(8,128)S(1)} %copy-done.14, f32[128,512]{1,0:T(8,128)} %get-tuple-element.76), channel_id=1, replica_groups=mesh['rows'=16,'cols'=2] {'rows'}, use_global_device_ids=true, to_apply=%region_6.9 | all-reduce | flops 196608 | bytes 1179648 | tf_op jit(solution)/shard_map/psum | solution.py:46
  146.6 31.8 %all-reduce.24.cloned.1.call-done = (f32[128,512]{1,0:T(8,128)}, f32[128,512]{1,0:T(8,128)}, f32[128,512]{1,0:T(8,128)}, f32[128,512]{1,0:T(8,128)}) async-done(((f32[128,512]{1,0:T(8,128)}, f32[128,512]{1,0:T(8,128)}, f32[128,512]{1,0:T(8,128)}, f32[128,512]{1,0:T(8,128)}), (f32[128,512]{1,0:T(8,128)}, f32[128,512]{1,0:T(8,128)}, f32[128,512]{1,0:T(8,128)}, ...) | async-done | bytes 1048592 | tf_op jit(solution)/shard_map/psum | solution.py:46
  181.0 11.7 %cholesky.74 = f32[128,128]{1,0:T(8,128)S(1)} custom-call(f32[128,128]{1,0:T(8,128)S(1)} %fusion.93), custom_call_target="Cholesky" | custom-call | tf_op jit(solution)/shard_map/jit(cholesky)/cholesky | solution.py:75
  194.0 9.8 %custom-call.8 = f32[1,128,128]{1,2,0:T(8,128)S(1)} custom-call(f32[1,128,128]{2,1,0:T(8,128)S(1)} %fusion.82), custom_call_target="InvertDiagBlocksLowerTriangular" | custom-call | tf_op jit(solution)/shard_map/triangular_solve/custom-call.0 | solution.py:76
  210.7 15.4 %all-reduce.30.cloned.1.call-done = (f32[128,1024]{1,0:T(8,128)}, f32[128,512]{1,0:T(8,128)}) async-done(((f32[128,1024]{1,0:T(8,128)}, f32[128,512]{1,0:T(8,128)}), (f32[128,1024]{1,0:T(8,128)}, f32[128,512]{1,0:T(8,128)})) %all-reduce.30.cloned.1.call-update) | async-done | bytes 786448 | tf_op jit(solution)/shard_map/psum | solution.py:46
  226.1 87.2 %all-reduce.34 = (bf16[128,1024]{1,0:T(8,128)(2,1)S(1)}, bf16[128,512]{1,0:T(8,128)(2,1)S(1)}) all-reduce(f32[128,1024]{1,0:T(8,128)} %get-tuple-element.73, f32[128,512]{1,0:T(8,128)} %get-tuple-element.74), channel_id=1, replica_groups=mesh['rows'=16,'cols'=2] {'rows'}, use_global_device_ids=true, to_apply=%region_16.21 | all-reduce | flops 196608 | bytes 1179648 | tf_op jit(solution)/shard_map/psum | solution.py:46
  318.8 13.2 %cholesky.85 = f32[128,128]{1,0:T(8,128)} custom-call(f32[128,128]{1,0:T(8,128)} %fusion.91), custom_call_target="Cholesky" | custom-call | tf_op jit(solution)/shard_map/jit(cholesky)/cholesky | solution.py:75
  333.5 2.1 fusion.83
  335.6 11.3 %custom-call.9 = f32[1,128,128]{1,2,0:T(8,128)} custom-call(f32[1,128,128]{2,1,0:T(8,128)} %fusion.83), custom_call_target="InvertDiagBlocksLowerTriangular" | custom-call | tf_op jit(solution)/shard_map/triangular_solve/custom-call.0 | solution.py:76
  354.4 12.6 %all-reduce.28.cloned.1.call-done = (f32[128,1024]{1,0:T(8,128)}, f32[128,512]{1,0:T(8,128)}) async-done(((f32[128,1024]{1,0:T(8,128)}, f32[128,512]{1,0:T(8,128)}), (f32[128,1024]{1,0:T(8,128)}, f32[128,512]{1,0:T(8,128)})) %all-reduce.28.cloned.1.call-update) | async-done | bytes 786448 | tf_op jit(solution)/shard_map/psum | solution.py:46
  367.0 86.8 %all-reduce.35 = (bf16[128,1024]{1,0:T(8,128)(2,1)S(1)}, bf16[128,512]{1,0:T(8,128)(2,1)}) all-reduce(f32[128,1024]{1,0:T(8,128)} %get-tuple-element.71, f32[128,512]{1,0:T(8,128)} %get-tuple-element.72), channel_id=1, replica_groups=mesh['rows'=16,'cols'=2] {'rows'}, use_global_device_ids=true, to_apply=%region_24.29 | all-reduce | flops 196608 | bytes 1179648 | tf_op jit(solution)/shard_map/psum | solution.py:46
  455.8 12.5 %cholesky.96 = f32[128,128]{1,0:T(8,128)S(1)} custom-call(f32[128,128]{1,0:T(8,128)} %fusion.89), custom_call_target="Cholesky" | custom-call | tf_op jit(solution)/shard_map/jit(cholesky)/cholesky | solution.py:75
  469.7 9.8 %custom-call.10 = f32[1,128,128]{1,2,0:T(8,128)S(1)} custom-call(f32[1,128,128]{2,1,0:T(8,128)S(1)} %fusion.84), custom_call_target="InvertDiagBlocksLowerTriangular" | custom-call | tf_op jit(solution)/shard_map/triangular_solve/custom-call.0 | solution.py:76
  483.8 15.3 %all-reduce.26.cloned.1.call-done = (f32[128,1024]{1,0:T(8,128)}, f32[128,512]{1,0:T(8,128)}) async-done(((f32[128,1024]{1,0:T(8,128)}, f32[128,512]{1,0:T(8,128)}), (f32[128,1024]{1,0:T(8,128)}, f32[128,512]{1,0:T(8,128)})) %all-reduce.26.cloned.1.call-update) | async-done | bytes 786448 | tf_op jit(solution)/shard_map/psum | solution.py:46
  499.1 86.8 %all-reduce.36 = (bf16[128,1024]{1,0:T(8,128)(2,1)S(1)}, bf16[128,512]{1,0:T(8,128)(2,1)}) all-reduce(f32[128,1024]{1,0:T(8,128)} %get-tuple-element.69, f32[128,512]{1,0:T(8,128)} %get-tuple-element.70), channel_id=1, replica_groups=mesh['rows'=16,'cols'=2] {'rows'}, use_global_device_ids=true, to_apply=%region_31.36 | all-reduce | flops 196608 | bytes 1179648 | tf_op jit(solution)/shard_map/psum | solution.py:46
  587.2 11.7 %cholesky.107 = f32[128,128]{1,0:T(8,128)S(1)} custom-call(f32[128,128]{1,0:T(8,128)S(1)} %fusion.87), custom_call_target="Cholesky" | custom-call | tf_op jit(solution)/shard_map/jit(cholesky)/cholesky | solution.py:75
  600.3 9.8 %custom-call.11 = f32[1,128,128]{1,2,0:T(8,128)S(1)} custom-call(f32[1,128,128]{2,1,0:T(8,128)S(1)} %fusion.85), custom_call_target="InvertDiagBlocksLowerTriangular" | custom-call | tf_op jit(solution)/shard_map/triangular_solve/custom-call.0 | solution.py:76
  612.5 5.8 all-gather.2.cloned.1.call-done
  619.5 3.5 fusion.63
  624.8 119.0 %all-reduce.22.cloned.1.call-done = (f32[512,512]{1,0:T(8,128)}, f32[512,256]{1,0:T(8,128)}) async-done(((f32[512,512]{1,0:T(8,128)}, f32[512,256]{1,0:T(8,128)}), (f32[512,512]{1,0:T(8,128)}, f32[512,256]{1,0:T(8,128)})) %all-reduce.22.cloned.1.call-update) | async-done | bytes 1572880 | tf_op jit(solution)/shard_map/psum | solution.py:86
  (164 shorter events, 61.8 us)
Async XLA Ops:
  7.2 3.6 copy-start.20
  7.2 3.6 copy-start.18
  7.2 5.4 all-to-all-start
  11.4 4.9 copy-start.25
  12.5 10.2 %all-to-all-start.1 = ((bf16[2,640,512]{2,1,0:T(8,128)(2,1)}), bf16[2,640,512]{2,1,0:T(8,128)(2,1)S(1)}, u32[]{:S(2)}, u32[]{:S(2)}) async-start(bf16[2,640,512]{2,1,0:T(8,128)(2,1)} %bitcast.251), calls=%async_computation.1 | async-start | bytes 2621440 | tf_op jit(solution)/shard_map/all_to_all | solution.py:24
  16.2 38.8 %all-reduce.32.cloned.1.call-start = ((), (), s32[]{:S(2)}) async-start(), calls=%async_computation.8 | async-start | bytes 3670016 | tf_op jit(solution)/shard_map/psum | solution.py:46
  21.9 3.4 copy-start.22
  25.3 2.7 copy-start.13
  30.8 147.5 %all-reduce.24.cloned.1.call-start = ((), (), s32[]{:S(2)}) async-start(), calls=%async_computation.4 | async-start | bytes 2097152 | tf_op jit(solution)/shard_map/psum | solution.py:46
  55.0 171.1 %all-reduce.30.cloned.1.call-start = ((), (), s32[]{:S(2)}) async-start(), calls=%async_computation.7 | async-start | bytes 1572864 | tf_op jit(solution)/shard_map/psum | solution.py:46
  178.3 25.9 %copy-start.5 = (f32[128,512]{1,0:T(8,128)S(1)}, f32[128,512]{1,0:T(8,128)}, u32[]{:S(2)}) copy-start(f32[128,512]{1,0:T(8,128)} %get-tuple-element.65) | copy-start | bytes 786436
  207.8 2.7 copy-start.4
  207.8 159.2 %all-reduce.28.cloned.1.call-start = ((), (), s32[]{:S(2)}) async-start(), calls=%async_computation.6 | async-start | bytes 1572864 | tf_op jit(solution)/shard_map/psum | solution.py:46
  314.7 33.3 %copy-start.7 = (f32[640,128]{1,0:T(8,128)S(1)}, f32[640,128]{1,0:T(8,128)}, u32[]{:S(2)}) copy-start(f32[640,128]{1,0:T(8,128)} %fusion.17) | copy-start | bytes 983044
  351.5 2.8 copy-start.3
  351.5 147.6 %all-reduce.26.cloned.1.call-start = ((), (), s32[]{:S(2)}) async-start(), calls=%async_computation.5 | async-start | bytes 1572864 | tf_op jit(solution)/shard_map/psum | solution.py:46
  454.8 25.3 %copy-start.11 = (bf16[128,512]{1,0:T(8,128)(2,1)S(1)}, bf16[128,512]{1,0:T(8,128)(2,1)}, u32[]{:S(2)}) copy-start(bf16[128,512]{1,0:T(8,128)(2,1)} %get-tuple-element.58) | copy-start | bytes 393220
  483.6 134.7 %all-gather.2.cloned.1.call-start = ((), (), s32[]{:S(2)}) async-start(), calls=%async_computation.2 | async-start | bytes 1966080 | tf_op jit(solution)/shard_map/all_gather | solution.py:79
  586.9 23.8 %copy-start.9 = (bf16[128,512]{1,0:T(8,128)(2,1)S(1)}, bf16[128,512]{1,0:T(8,128)(2,1)}, u32[]{:S(2)}) copy-start(bf16[128,512]{1,0:T(8,128)(2,1)} %get-tuple-element.56) | copy-start | bytes 393220
  611.1 8.4 %copy-start.6 = (bf16[1280,512]{1,0:T(8,128)(2,1)S(1)}, bf16[1280,512]{1,0:T(8,128)(2,1)}, u32[]{:S(2)}) copy-start(bf16[1280,512]{1,0:T(8,128)(2,1)} %param.21) | copy-start | bytes 3932164
  611.1 8.4 %copy-start.26 = (f32[1280]{0:T(1024)S(1)}, f32[1280]{0:T(1024)}, u32[]{:S(2)}) copy-start(f32[1280]{0:T(1024)} %param.22) | copy-start | bytes 15364
  612.5 131.3 %all-reduce.22.cloned.1.call-start = ((), (), s32[]{:S(2)}) async-start(), calls=%async_computation.3 | async-start | bytes 3145728 | tf_op jit(solution)/shard_map/psum | solution.py:86
  619.5 3.6 copy-start.12
  619.5 3.6 copy-start.15
  (12 other events, 13.8 us)
Sparse Core Ops, SparseCore 0:
  30.9 24.0 all-reduce.31
  60.7 117.6 all-reduce.23
  207.9 18.0 all-reduce.29
  351.7 15.3 all-reduce.27
  483.7 15.3 all-reduce.25
  612.6 5.7 all-gather.1
  624.9 118.8 all-reduce.21
